TPU v7x, 32 devices: a whole 2x2x4 slice. The times are simulated.
32 devices in a mesh: rep: 8 (over z, x), shard: 4 (over y, core).
Axes of the slice: x: 2, y: 2, z: 4, core: 2. Of those that a mesh axis runs over, the one named last changes fastest.
Arguments:
- grads: bfloat16 [8, 12, 512, 512], P('rep', 'shard')
- owner_slot: int32 [12], replicated, may hold values from 0 to 11, as said below
- refresh: int32 [1], replicated, may hold values from 0 to 11
- left_stat: float32 [12, 512, 512], P('shard', 'rep'), as said below
- right_stat: float32 [12, 512, 512], P('shard', 'rep'), as said below
- left_root: bfloat16 [12, 512, 512], P('shard', 'rep'), as said below
- right_root: bfloat16 [12, 512, 512], P('shard'), as said below
Outputs:
- left_new: float32 [12, 512, 512], P('shard', 'rep')
- right_new: float32 [12, 512, 512], P('shard', 'rep')
- left_root_new: bfloat16 [12, 512, 512], P('shard', 'rep')
- right_root_new: bfloat16 [12, 512, 512], P('shard')
- direction: bfloat16 [12, 512, 512], P('shard')
Inputs may be any that keep to these rules, and one draw needn't show every extreme that they name: A permutation: block b sits at position owner_slot[b] of owner order, which belongs to shard index owner_slot[b] // 3, with owner_slot[b] % 3 == b % 3; the 3 blocks s * 3 to s * 3 + 2 all go to different shard indices. `left_stat`: each block is symmetric positive definite. `right_stat`: each block is symmetric positive definite. `left_root`: each block is symmetric. `right_root`: each block is symmetric.
All inputs are finite; a program needn't handle non-finite values.
Results may differ from a plain program's by a relative error of at most 0.0004.
The roundings to bfloat16 on the way count: a program that leaves them out, or rounds other values in their place, can miss the bound.
Values may be sent and summed in bfloat16 or wider, within the bound.
A program may use at most 64 MiB of HBM per device.

v0:
```python
import jax
import jax.numpy as jnp
from jax import lax
from jax.sharding import PartitionSpec as P

ITERS = 2
decay_rate = 0.95
epsilon_shift = 1e-06


def inverse_root(statistic):
    order = statistic.shape[0]
    identity = jnp.eye(order, dtype=jnp.float32)
    shifted = statistic + epsilon_shift * identity
    norm_scale = 2.5 / jnp.sqrt(jnp.sum(shifted * shifted))
    moment = norm_scale * shifted
    current = identity
    for number in range(ITERS):
        factor = (5.0 * identity - moment) * 0.25
        factor_low = factor.astype(jnp.bfloat16)
        if number == 0:
            current = jnp.sqrt(jnp.sqrt(norm_scale)) * factor
        else:
            current = jnp.dot(
                current.astype(jnp.bfloat16), factor_low, preferred_element_type=jnp.float32
            )
        if number + 1 < ITERS:
            square = jnp.dot(factor_low, factor_low, preferred_element_type=jnp.float32).astype(
                jnp.bfloat16
            )
            fourth = jnp.dot(square, square, preferred_element_type=jnp.float32).astype(
                jnp.bfloat16
            )
            moment = jnp.dot(
                fourth, moment.astype(jnp.bfloat16), preferred_element_type=jnp.float32
            )
    return current.astype(jnp.bfloat16)


def both_roots(fresh_whole):
    return (inverse_root(fresh_whole[0]), inverse_root(fresh_whole[1]))


def empty_roots(fresh_whole):
    blank = jnp.zeros(fresh_whole.shape[1:], jnp.bfloat16)
    return (blank, blank)


def body(grads, owner_slot, refresh, left_stat, right_stat, left_root, right_root):
    blocks = grads.shape[1]
    block_order = grads.shape[2]
    rep_count = lax.axis_size("rep")
    shards = lax.axis_size("shard")
    row_count = block_order // rep_count
    rep_index = lax.axis_index("rep")
    shard_index = lax.axis_index("shard")
    partial_value = grads[0].astype(jnp.float32)
    row_share = lax.psum_scatter(partial_value, "rep", scatter_dimension=1, tiled=True)
    row_share = row_share.astype(jnp.bfloat16)
    slot_table = owner_slot.reshape(shards, blocks)
    own_slots = lax.dynamic_index_in_dim(slot_table, shard_index, 0, keepdims=False)
    targets = own_slots // blocks
    selector = (targets[None, :] == jnp.arange(shards, dtype=jnp.int32)[:, None]).astype(
        jnp.bfloat16
    )
    outgoing = jnp.einsum(
        "ok,krc->orc", selector, row_share, preferred_element_type=jnp.float32
    ).astype(jnp.bfloat16)
    incoming = lax.all_to_all(outgoing, "shard", split_axis=0, concat_axis=0, tiled=True)
    wanted = shard_index * blocks + jnp.arange(blocks, dtype=jnp.int32)
    receiver = (jnp.transpose(slot_table) == wanted[:, None]).astype(jnp.bfloat16)
    owned_rows = jnp.einsum(
        "ks,src->krc", receiver, incoming, preferred_element_type=jnp.float32
    ).astype(jnp.bfloat16)
    gathered = lax.all_gather(owned_rows, "rep", axis=1, tiled=True)
    left_new = (
        decay_rate * left_stat
        + jnp.einsum("krc,kjc->krj", owned_rows, gathered, preferred_element_type=jnp.float32)
        / block_order
    )
    column_share = lax.dynamic_slice_in_dim(gathered, rep_index * row_count, row_count, 2)
    right_new = (
        decay_rate * right_stat
        + jnp.einsum("kic,kij->kcj", column_share, gathered, preferred_element_type=jnp.float32)
        / block_order
    )
    fresh_slot = owner_slot[refresh[0]]
    holder = fresh_slot // blocks
    slot_index = fresh_slot % blocks
    owns_fresh = holder == shard_index
    fresh_pair = jnp.stack(
        [
            lax.dynamic_index_in_dim(left_new, slot_index, 0, keepdims=False),
            lax.dynamic_index_in_dim(right_new, slot_index, 0, keepdims=False),
        ]
    )
    fresh_whole = lax.all_gather(fresh_pair, "rep", axis=1, tiled=True)
    fresh_left, fresh_right = lax.cond(owns_fresh, both_roots, empty_roots, fresh_whole)
    fresh_rows = lax.dynamic_slice_in_dim(fresh_left, rep_index * row_count, row_count, 0)
    left_updated = lax.dynamic_update_index_in_dim(left_root, fresh_rows, slot_index, 0)
    left_root_new = jnp.where(owns_fresh, left_updated, left_root)
    right_updated = lax.dynamic_update_index_in_dim(right_root, fresh_right, slot_index, 0)
    right_root_new = jnp.where(owns_fresh, right_updated, right_root)
    half_step = jnp.einsum(
        "kri,kic->krc", left_root_new, gathered, preferred_element_type=jnp.float32
    ).astype(jnp.bfloat16)
    preconditioned = jnp.einsum(
        "kri,kic->krc", half_step, right_root_new, preferred_element_type=jnp.float32
    ).astype(jnp.bfloat16)
    direction = lax.all_gather(preconditioned, "rep", axis=1, tiled=True)
    return (left_new, right_new, left_root_new, right_root_new, direction)


def solution(mesh):
    return jax.shard_map(
        body,
        mesh=mesh,
        in_specs=(
            P("rep", "shard", None, None),
            P(),
            P(),
            P("shard", "rep", None),
            P("shard", "rep", None),
            P("shard", "rep", None),
            P("shard", None, None),
        ),
        out_specs=(
            P("shard", "rep", None),
            P("shard", "rep", None),
            P("shard", "rep", None),
            P("shard", None, None),
            P("shard", None, None),
        ),
        check_vma=False,
    )
```

profile of v0, /device:TPU:0, one launch (start us, length us, event | category | flops | bytes accessed | tf_op | source)
XLA Modules:
  0.0 272.0 jit_solution(3963300385175303924)
XLA Ops:
  7.2 1.4 copy-done.3
  8.6 2.1 bitcast_convert_fusion
  10.7 0.6 copy-done.10
  11.4 77.7 %reduce-scatter.2.cloned.1.call-done = f32[3,64,512]{2,1,0:T(8,128)} async-done(((f32[3,512,512]{2,1,0:T(8,128)}), f32[3,64,512]{2,1,0:T(8,128)}) %reduce-scatter.2.cloned.1.call-update) | async-done | bytes 393232 | tf_op jit(solution)/shard_map/reduce_scatter | solution.py:58
  89.1 1.0 convert_element_type.80
  90.4 0.7 copy.23
  91.2 3.4 %all-to-all-start = ((bf16[4,64,512]{2,1,0:T(8,128)(2,1)}), bf16[4,64,512]{2,1,0:T(8,128)(2,1)S(1)}, u32[]{:S(2)}, u32[]{:S(2)}) async-start(bf16[4,64,512]{2,1,0:T(8,128)(2,1)} %copy.23), calls=%async_computation.1 | async-start | bytes 524288 | tf_op jit(solution)/shard_map/all_to_all | solution.py:69
  94.7 5.9 %all-to-all-done = bf16[4,64,512]{2,1,0:T(8,128)(2,1)S(1)} async-done(((bf16[4,64,512]{2,1,0:T(8,128)(2,1)}), bf16[4,64,512]{2,1,0:T(8,128)(2,1)S(1)}, u32[]{:S(2)}, u32[]{:S(2)}) %all-to-all-start) | async-done | bytes 262176 | tf_op jit(solution)/shard_map/all_to_all | solution.py:69
  101.0 0.7 copy.36
  102.4 0.6 dynamic_slice.22
  103.7 40.6 %all-gather.4.cloned.1.call-done = bf16[3,512,512]{2,1,0:T(8,128)(2,1)} async-done(((bf16[3,64,512]{2,1,0:T(8,128)(2,1)}), bf16[3,512,512]{2,1,0:T(8,128)(2,1)}) %all-gather.4.cloned.1.call-update) | async-done | bytes 1572880 | tf_op jit(solution)/shard_map/all_gather | solution.py:75
  144.2 2.2 fusion.90
  146.5 0.5 fusion.89
  147.2 0.7 copy-done.7
  148.0 0.7 pad_maximum_fusion
  150.1 46.2 %all-gather.6.cloned.1.call-done = f32[2,512,512]{2,1,0:T(8,128)} async-done(((f32[2,64,512]{2,1,0:T(8,128)}), f32[2,512,512]{2,1,0:T(8,128)}) %all-gather.6.cloned.1.call-update) | async-done | bytes 2097168 | tf_op jit(solution)/shard_map/all_gather | solution.py:97
  196.3 1.7 conditional.1
  196.3 0.8 broadcast.90
  197.1 0.8 broadcast_in_dim.12
  198.2 0.7 copy-done.5
  198.9 0.9 fusion.95
  199.8 1.3 convolution_convert_fusion.7
  201.1 61.7 %all-gather.8.cloned.1.call-done = bf16[3,512,512]{2,1,0:T(8,128)(2,1)} async-done(((bf16[3,64,512]{2,1,0:T(8,128)(2,1)}), bf16[3,512,512]{2,1,0:T(8,128)(2,1)}) %all-gather.8.cloned.1.call-update) | async-done | bytes 1572880 | tf_op jit(solution)/shard_map/all_gather | solution.py:110
  262.8 2.7 copy.49
  (33 shorter events, 1.4 us)
Async XLA Ops:
  7.2 1.4 copy-start.3
  7.2 81.9 %reduce-scatter.2.cloned.1.call-start = ((), (), s32[]{:S(2)}) async-start(), calls=%async_computation.2 | async-start | bytes 3538944 | tf_op jit(solution)/shard_map/reduce_scatter | solution.py:58
  10.7 0.7 copy-start.10
  90.1 54.1 %copy-start.8 = (f32[3,64,512]{2,1,0:T(8,128)S(1)}, f32[3,64,512]{2,1,0:T(8,128)}, u32[]{:S(2)}) copy-start(f32[3,64,512]{2,1,0:T(8,128)} %param.12) | copy-start | bytes 1179652
  91.2 9.4 %all-to-all-start = ((bf16[4,64,512]{2,1,0:T(8,128)(2,1)}), bf16[4,64,512]{2,1,0:T(8,128)(2,1)S(1)}, u32[]{:S(2)}, u32[]{:S(2)}) async-start(bf16[4,64,512]{2,1,0:T(8,128)(2,1)} %copy.23), calls=%async_computation.1 | async-start | bytes 524288 | tf_op jit(solution)/shard_map/all_to_all | solution.py:69
  94.6 49.6 %all-gather.4.cloned.1.call-start = ((), (), s32[]{:S(2)}) async-start(), calls=%async_computation.3 | async-start | bytes 1769472 | tf_op jit(solution)/shard_map/all_gather | solution.py:75
  100.9 45.5 %copy-start.9 = (f32[3,64,512]{2,1,0:T(8,128)S(1)}, f32[3,64,512]{2,1,0:T(8,128)}, u32[]{:S(2)}) copy-start(f32[3,64,512]{2,1,0:T(8,128)} %param.13) | copy-start | bytes 1179652
  101.7 94.6 %all-gather.6.cloned.1.call-start = ((), (), s32[]{:S(2)}) async-start(), calls=%async_computation.4 | async-start | bytes 2359296 | tf_op jit(solution)/shard_map/all_gather | solution.py:97
  144.2 2.2 copy-start
  146.5 0.7 copy-start.6
  147.2 0.7 copy-start.7
  148.7 114.1 %all-gather.8.cloned.1.call-start = ((), (), s32[]{:S(2)}) async-start(), calls=%async_computation.5 | async-start | bytes 1769472 | tf_op jit(solution)/shard_map/all_gather | solution.py:110
  150.1 47.9 %copy-start.2 = (bf16[3,512,512]{2,1,0:T(8,128)(2,1)S(1)}, bf16[3,512,512]{2,1,0:T(8,128)(2,1)}, u32[]{:S(2)}) copy-start(bf16[3,512,512]{2,1,0:T(8,128)(2,1)} %param.15) | copy-start | bytes 4718596
  198.0 0.9 copy-start.5
  198.1 3.0 %copy-start.1 = (bf16[3,512,512]{2,1,0:T(8,128)(2,1)}, bf16[3,512,512]{2,1,0:T(8,128)(2,1)S(1)}, u32[]{:S(2)}) copy-start(bf16[3,512,512]{2,1,0:T(8,128)(2,1)S(1)} %select_dynamic-update-slice_fusion) | copy-start | bytes 4718596
  199.7 1.4 copy-start.4
Sparse Core Ops, SparseCore 0:
  11.6 77.4 reduce-scatter.1
  101.8 42.3 all-gather.3
  148.8 47.4 all-gather.5
  201.2 61.5 all-gather.7
where the time goes:
time: 273 us; the launch traced here: 272 us
  waiting for transfers between devices  232 us (85%)
  between operations  16.5 us (6%)
  local copies, waits for them, and re-layouts  10.1 us (4%)
  other arithmetic  4.88 us (2%)
  matrix products  4.75 us (2%)
  starting transfers between devices  3.57 us (1%)
    reduce_scatter x1, waiting for transfers between devices, body(): lax.psum_scatter(partial_value, 'rep', scatter_dimension=1, tiled=True)  77.7 us
    all_gather x1, waiting for transfers between devices, body(): direction = lax.all_gather(preconditioned, 'rep', axis=1, tiled=True)  61.7 us
    all_gather x1, waiting for transfers between devices, body(): fresh_whole = lax.all_gather(fresh_pair, 'rep', axis=1, tiled=True)  46.2 us
    all_gather x1, waiting for transfers between devices, body(): gathered = lax.all_gather(owned_rows, 'rep', axis=1, tiled=True)  40.6 us
    unnamed x23, local copies, waits for them, and re-layouts  6.3 us
    all_to_all x1, waiting for transfers between devices, body(): lax.all_to_all(outgoing, 'shard', split_axis=0, concat_axis=0, tiled=True)  5.91 us
  transfers between devices with their start and end apart: 5, of which 5 were waited for; matrix products, arithmetic and copies ran while one was open for 0% of the time, Pallas kernels for 0%

commit v1 on v0

--- a/solution.py
+++ b/solution.py
@@ -6,6 +6,20 @@
 ITERS = 2
 decay_rate = 0.95
 epsilon_shift = 1e-06
+
+
+def obtain_face(a0):
+    nd = jax.lax.axis_size("rep")
+    known = a0
+    u_next = sorted(((dev_j, (dev_j + 1) % nd) for dev_j in range(nd)))
+    kept_rows = [known]
+    for num in range(1, nd):
+        known = jax.lax.ppermute(known, "rep", u_next)
+        kept_rows.insert(0, known)
+    met_up = jnp.concatenate(kept_rows, axis=1)
+    block_next = jax.lax.axis_index("rep")
+    current_block = block_next + 1
+    return jnp.roll(met_up, current_block * a0.shape[1], axis=1)
 
 
 def inverse_root(statistic):
@@ -72,7 +86,7 @@
     owned_rows = jnp.einsum(
         "ks,src->krc", receiver, incoming, preferred_element_type=jnp.float32
     ).astype(jnp.bfloat16)
-    gathered = lax.all_gather(owned_rows, "rep", axis=1, tiled=True)
+    gathered = obtain_face(owned_rows)
     left_new = (
         decay_rate * left_stat
         + jnp.einsum("krc,kjc->krj", owned_rows, gathered, preferred_element_type=jnp.float32)

time: 273 us -> 296 us (1.084)
  waiting for transfers between devices: 232 us -> 251 us
    ppermute x0 -> x7, waiting for transfers between devices: none -> 63.9 us  [obtain_face(): known = jax.lax.ppermute(known, 'rep', u_next)]
    all_gather x1 -> x0, waiting for transfers between devices: 40.6 us -> none  [body(): gathered = lax.all_gather(owned_rows, 'rep', axis=1, tiled=True)]
    unnamed x23 -> x33, local copies, waits for them, and re-layouts: 6.3 us -> 7.13 us
  transfers between devices with their start and end apart: 5 -> 11, of which waited for: 5 -> 11; matrix products, arithmetic and copies ran while one was open for 0% -> 0% of each run, Pallas kernels for 0% -> 0%
where the time goes in v1:
time: 296 us; the launch traced here: 295 us
  waiting for transfers between devices  251 us (85%)
  between operations  16.6 us (6%)
  local copies, waits for them, and re-layouts  10.7 us (4%)
  other arithmetic  6.77 us (2%)
  matrix products  5 us (2%)
  starting transfers between devices  4.97 us (2%)
    reduce_scatter x1, waiting for transfers between devices, body(): lax.psum_scatter(partial_value, 'rep', scatter_dimension=1, tiled=True)  77.5 us
    ppermute x7, waiting for transfers between devices, obtain_face(): known = jax.lax.ppermute(known, 'rep', u_next)  63.9 us
    all_gather x1, waiting for transfers between devices, body(): direction = lax.all_gather(preconditioned, 'rep', axis=1, tiled=True)  60 us
    all_gather x1, waiting for transfers between devices, body(): fresh_whole = lax.all_gather(fresh_pair, 'rep', axis=1, tiled=True)  43.8 us
    unnamed x33, local copies, waits for them, and re-layouts  7.13 us
  transfers between devices with their start and end apart: 11, of which 11 were waited for; matrix products, arithmetic and copies ran while one was open for 0% of the time, Pallas kernels for 0%

profile of v1, /device:TPU:0, one launch (start us, length us, event | category | flops | bytes accessed | tf_op | source)
XLA Modules:
  0.0 295.1 jit_solution(547693028638205538)
XLA Ops:
  7.2 2.8 copy.70
  10.0 2.1 bitcast_convert_fusion
  12.2 77.5 %reduce-scatter.2.cloned.1.call-done = f32[3,64,512]{2,1,0:T(8,128)} async-done(((f32[3,512,512]{2,1,0:T(8,128)}), f32[3,64,512]{2,1,0:T(8,128)}) %reduce-scatter.2.cloned.1.call-update) | async-done | bytes 393232 | tf_op jit(solution)/shard_map/reduce_scatter | solution.py:72
  89.7 1.0 convert_element_type.80
  91.0 0.7 copy.43
  91.8 3.4 %all-to-all-start = ((bf16[4,64,512]{2,1,0:T(8,128)(2,1)}), bf16[4,64,512]{2,1,0:T(8,128)(2,1)S(1)}, u32[]{:S(2)}, u32[]{:S(2)}) async-start(bf16[4,64,512]{2,1,0:T(8,128)(2,1)} %copy.43), calls=%async_computation.1 | async-start | bytes 524288 | tf_op jit(solution)/shard_map/all_to_all | solution.py:83
  95.3 5.9 %all-to-all-done = bf16[4,64,512]{2,1,0:T(8,128)(2,1)S(1)} async-done(((bf16[4,64,512]{2,1,0:T(8,128)(2,1)}), bf16[4,64,512]{2,1,0:T(8,128)(2,1)S(1)}, u32[]{:S(2)}, u32[]{:S(2)}) %all-to-all-start) | async-done | bytes 262176 | tf_op jit(solution)/shard_map/all_to_all | solution.py:83
  101.5 1.4 collective-permute-start
  103.0 9.1 %collective-permute-done = bf16[3,64,512]{2,0,1:T(4,128)(2,1)S(1)} collective-permute-done((bf16[3,64,512]{2,0,1:T(4,128)(2,1)S(1)}, bf16[3,64,512]{2,0,1:T(4,128)(2,1)S(1)}, u32[]{:S(2)}, u32[]{:S(2)}) %collective-permute-start) | collective-permute-done | bytes 196640 | tf_op jit(solution)/shard_map/ppermute | solution.py:17
  112.0 9.6 %collective-permute-done.1 = bf16[3,64,512]{2,0,1:T(4,128)(2,1)S(1)} collective-permute-done((bf16[3,64,512]{2,0,1:T(4,128)(2,1)S(1)}, bf16[3,64,512]{2,0,1:T(4,128)(2,1)S(1)}, u32[]{:S(2)}, u32[]{:S(2)}) %collective-permute-start.1) | collective-permute-done | bytes 196640 | tf_op jit(solution)/shard_map/ppermute | solution.py:17
  121.6 9.1 %collective-permute-done.2 = bf16[3,64,512]{2,0,1:T(4,128)(2,1)S(1)} collective-permute-done((bf16[3,64,512]{2,0,1:T(4,128)(2,1)S(1)}, bf16[3,64,512]{2,0,1:T(4,128)(2,1)S(1)}, u32[]{:S(2)}, u32[]{:S(2)}) %collective-permute-start.2) | collective-permute-done | bytes 196640 | tf_op jit(solution)/shard_map/ppermute | solution.py:17
  130.7 9.1 %collective-permute-done.3 = bf16[3,64,512]{2,0,1:T(4,128)(2,1)S(1)} collective-permute-done((bf16[3,64,512]{2,0,1:T(4,128)(2,1)S(1)}, bf16[3,64,512]{2,0,1:T(4,128)(2,1)S(1)}, u32[]{:S(2)}, u32[]{:S(2)}) %collective-permute-start.3) | collective-permute-done | bytes 196640 | tf_op jit(solution)/shard_map/ppermute | solution.py:17
  139.8 9.4 %collective-permute-done.4 = bf16[3,64,512]{2,0,1:T(4,128)(2,1)S(1)} collective-permute-done((bf16[3,64,512]{2,0,1:T(4,128)(2,1)S(1)}, bf16[3,64,512]{2,0,1:T(4,128)(2,1)S(1)}, u32[]{:S(2)}, u32[]{:S(2)}) %collective-permute-start.4) | collective-permute-done | bytes 196640 | tf_op jit(solution)/shard_map/ppermute | solution.py:17
  149.2 10.5 %collective-permute-done.5 = bf16[3,64,512]{2,0,1:T(4,128)(2,1)S(1)} collective-permute-done((bf16[3,64,512]{2,0,1:T(4,128)(2,1)S(1)}, bf16[3,64,512]{2,0,1:T(4,128)(2,1)S(1)}, u32[]{:S(2)}, u32[]{:S(2)}) %collective-permute-start.5) | collective-permute-done | bytes 196640 | tf_op jit(solution)/shard_map/ppermute | solution.py:17
  161.6 7.1 %collective-permute-done.6 = bf16[3,64,512]{2,0,1:T(4,128)(2,1)S(1)} collective-permute-done((bf16[3,64,512]{2,0,1:T(4,128)(2,1)S(1)}, bf16[3,64,512]{2,0,1:T(4,128)(2,1)S(1)}, u32[]{:S(2)}, u32[]{:S(2)}) %collective-permute-start.6) | collective-permute-done | bytes 196640 | tf_op jit(solution)/shard_map/ppermute | solution.py:17
  173.2 0.8 pad_maximum_fusion
  175.4 43.8 %all-gather.3.cloned.1.call-done = f32[2,512,512]{2,1,0:T(8,128)} async-done(((f32[2,64,512]{2,1,0:T(8,128)}), f32[2,512,512]{2,1,0:T(8,128)}) %all-gather.3.cloned.1.call-update) | async-done | bytes 2097168 | tf_op jit(solution)/shard_map/all_gather | solution.py:111
  219.2 0.9 conditional.1
  219.2 0.8 broadcast.92
  220.1 2.0 select_dynamic-update-slice_fusion
  222.0 0.9 fusion.100
  222.9 3.0 %convolution_convert_fusion.7 = bf16[3,64,512]{2,1,0:T(8,128)(2,1)} fusion(bf16[3,512,512]{2,1,0:T(8,128)(2,1)} %select_dynamic-update-slice_fusion, bf16[3,64,512]{2,1,0:T(8,128)(2,1)S(1)} %fusion.100, bf16[3,512,512]{2,0,1:T(4,128)(2,1)S(1)} %constant_dynamic-slice_fusion.3), kind=kOutput, calls=%fused_computation.83 | convolution fusion | flops 201523200 | bytes 3538944 | tf_op jit(solution)/shard_map/kri,kic->krc/dot_general | solution.py:121
  226.0 60.0 %all-gather.5.cloned.1.call-done = bf16[3,512,512]{2,1,0:T(8,128)(2,1)} async-done(((bf16[3,64,512]{2,1,0:T(8,128)(2,1)}), bf16[3,512,512]{2,1,0:T(8,128)(2,1)}) %all-gather.5.cloned.1.call-update) | async-done | bytes 1572880 | tf_op jit(solution)/shard_map/all_gather | solution.py:124
  285.9 2.7 copy.71
  (56 shorter events, 5.9 us)
Async XLA Ops:
  7.2 2.8 copy-start
  7.2 82.5 %reduce-scatter.2.cloned.1.call-start = ((), (), s32[]{:S(2)}) async-start(), calls=%async_computation.2 | async-start | bytes 3538944 | tf_op jit(solution)/shard_map/reduce_scatter | solution.py:72
  10.0 2.1 copy-start.7
  91.8 9.4 %all-to-all-start = ((bf16[4,64,512]{2,1,0:T(8,128)(2,1)}), bf16[4,64,512]{2,1,0:T(8,128)(2,1)S(1)}, u32[]{:S(2)}, u32[]{:S(2)}) async-start(bf16[4,64,512]{2,1,0:T(8,128)(2,1)} %copy.43), calls=%async_computation.1 | async-start | bytes 524288 | tf_op jit(solution)/shard_map/all_to_all | solution.py:83
  95.2 124.0 %all-gather.3.cloned.1.call-start = ((), (), s32[]{:S(2)}) async-start(), calls=%async_computation.3 | async-start | bytes 2359296 | tf_op jit(solution)/shard_map/all_gather | solution.py:111
  101.5 10.5 %collective-permute-start = (bf16[3,64,512]{2,0,1:T(4,128)(2,1)S(1)}, bf16[3,64,512]{2,0,1:T(4,128)(2,1)S(1)}, u32[]{:S(2)}, u32[]{:S(2)}) collective-permute-start(bf16[3,64,512]{2,0,1:T(4,128)(2,1)S(1)} %convolution_convert_fusion.6), channel_id=1, source_target_pairs={{0,4},{4,8},{8,12},{12,16},{16,20},{20,24},{24,28},{28,0},{1,5},{5... | collective-permute-start | bytes 589832 | tf_op jit(solution)/shard_map/ppermute | solution.py:17
  112.0 9.6 %collective-permute-start.1 = (bf16[3,64,512]{2,0,1:T(4,128)(2,1)S(1)}, bf16[3,64,512]{2,0,1:T(4,128)(2,1)S(1)}, u32[]{:S(2)}, u32[]{:S(2)}) collective-permute-start(bf16[3,64,512]{2,0,1:T(4,128)(2,1)S(1)} %collective-permute-done), channel_id=1, source_target_pairs={{0,4},{4,8},{8,12},{12,16},{16,20},{20,24},{24,28},{28,0},{1,5},{5... | collective-permute-start | bytes 589832 | tf_op jit(solution)/shard_map/ppermute | solution.py:17
  121.6 9.1 %collective-permute-start.2 = (bf16[3,64,512]{2,0,1:T(4,128)(2,1)S(1)}, bf16[3,64,512]{2,0,1:T(4,128)(2,1)S(1)}, u32[]{:S(2)}, u32[]{:S(2)}) collective-permute-start(bf16[3,64,512]{2,0,1:T(4,128)(2,1)S(1)} %collective-permute-done.1), channel_id=1, source_target_pairs={{0,4},{4,8},{8,12},{12,16},{16,20},{20,24},{24,28},{28,0},{1,5},{5... | collective-permute-start | bytes 589832 | tf_op jit(solution)/shard_map/ppermute | solution.py:17
  130.7 9.1 %collective-permute-start.3 = (bf16[3,64,512]{2,0,1:T(4,128)(2,1)S(1)}, bf16[3,64,512]{2,0,1:T(4,128)(2,1)S(1)}, u32[]{:S(2)}, u32[]{:S(2)}) collective-permute-start(bf16[3,64,512]{2,0,1:T(4,128)(2,1)S(1)} %collective-permute-done.2), channel_id=1, source_target_pairs={{0,4},{4,8},{8,12},{12,16},{16,20},{20,24},{24,28},{28,0},{1,5},{5... | collective-permute-start | bytes 589832 | tf_op jit(solution)/shard_map/ppermute | solution.py:17
  139.8 9.4 %collective-permute-start.4 = (bf16[3,64,512]{2,0,1:T(4,128)(2,1)S(1)}, bf16[3,64,512]{2,0,1:T(4,128)(2,1)S(1)}, u32[]{:S(2)}, u32[]{:S(2)}) collective-permute-start(bf16[3,64,512]{2,0,1:T(4,128)(2,1)S(1)} %collective-permute-done.3), channel_id=1, source_target_pairs={{0,4},{4,8},{8,12},{12,16},{16,20},{20,24},{24,28},{28,0},{1,5},{5... | collective-permute-start | bytes 589832 | tf_op jit(solution)/shard_map/ppermute | solution.py:17
  149.2 10.5 %collective-permute-start.5 = (bf16[3,64,512]{2,0,1:T(4,128)(2,1)S(1)}, bf16[3,64,512]{2,0,1:T(4,128)(2,1)S(1)}, u32[]{:S(2)}, u32[]{:S(2)}) collective-permute-start(bf16[3,64,512]{2,0,1:T(4,128)(2,1)S(1)} %collective-permute-done.4), channel_id=1, source_target_pairs={{0,4},{4,8},{8,12},{12,16},{16,20},{20,24},{24,28},{28,0},{1,5},{5... | collective-permute-start | bytes 589832 | tf_op jit(solution)/shard_map/ppermute | solution.py:17
  159.7 9.1 %collective-permute-start.6 = (bf16[3,64,512]{2,0,1:T(4,128)(2,1)S(1)}, bf16[3,64,512]{2,0,1:T(4,128)(2,1)S(1)}, u32[]{:S(2)}, u32[]{:S(2)}) collective-permute-start(bf16[3,64,512]{2,0,1:T(4,128)(2,1)S(1)} %collective-permute-done.5), channel_id=1, source_target_pairs={{0,4},{4,8},{8,12},{12,16},{16,20},{20,24},{24,28},{28,0},{1,5},{5... | collective-permute-start | bytes 589832 | tf_op jit(solution)/shard_map/ppermute | solution.py:17
  169.9 1.9 copy-start.5
  170.5 1.9 copy-start.6
  172.5 46.7 %copy-start.3 = (f32[3,64,512]{2,1,0:T(8,128)}, f32[3,64,512]{2,1,0:T(8,128)S(1)}, u32[]{:S(2)}) copy-start(f32[3,64,512]{2,1,0:T(8,128)S(1)} %fusion.90) | copy-start | bytes 1179652
  173.2 46.0 %copy-start.4 = (f32[3,64,512]{2,1,0:T(8,128)}, f32[3,64,512]{2,1,0:T(8,128)S(1)}, u32[]{:S(2)}) copy-start(f32[3,64,512]{2,1,0:T(8,128)S(1)} %fusion.89) | copy-start | bytes 1179652
  174.0 111.9 %all-gather.5.cloned.1.call-start = ((), (), s32[]{:S(2)}) async-start(), calls=%async_computation.4 | async-start | bytes 1769472 | tf_op jit(solution)/shard_map/all_gather | solution.py:124
  175.4 46.7 %copy-start.2 = (bf16[3,64,512]{2,1,0:T(8,128)(2,1)S(1)}, bf16[3,64,512]{2,1,0:T(8,128)(2,1)}, u32[]{:S(2)}) copy-start(bf16[3,64,512]{2,1,0:T(8,128)(2,1)} %param.14) | copy-start | bytes 589828
  222.9 65.7 %copy-start.1 = (bf16[3,64,512]{2,1,0:T(8,128)(2,1)}, bf16[3,64,512]{2,1,0:T(8,128)(2,1)S(1)}, u32[]{:S(2)}) copy-start(bf16[3,64,512]{2,1,0:T(8,128)(2,1)S(1)} %fusion.100) | copy-start | bytes 589828
Sparse Core Ops, SparseCore 0:
  12.2 77.4 reduce-scatter.1
  174.1 44.9 all-gather.2
  226.1 59.8 all-gather.4
